TPU v7x, 256 devices: a whole 4x4x8 slice. The times are simulated.
256 devices in a mesh: row: 16 (over z, core), col: 8 (over x, y_lo), vec: 2 (over y_hi).
Axes of the slice: x: 4, y: 4 (y_hi: 2, y_lo: 2; y = y_hi * 2 + y_lo), z: 8, core: 2. Of those that a mesh axis runs over, the one named last changes fastest.
Arguments:
- vectors: bfloat16 [16, 131072], P('vec', ('row', 'col')), may hold values from -6 to 6
- tile_vals: bfloat16 [16, 8, 256, 128, 128], P('row', 'col'), may hold values from -0.09375 to 0.09375
- tile_rows: int32 [16, 8, 256], P('row', 'col'), may hold values from 0 to 1023, as said below
- tile_cols: int32 [16, 8, 256], P('row', 'col'), may hold values from 0 to 1023, as said below
- tile_counts: int32 [16, 8], P('row', 'col'), may hold values from 1 to 256, as said below
Outputs:
- product: bfloat16 [16, 131072], P('vec', ('row', 'col'))
- gram: float32 [16, 16], P(None, 'vec')
Inputs may be any that keep to these rules, and one draw needn't show every extreme that they name: `tile_rows`: list [i, j] names tiles whose row index r has i * 64 <= r < (i + 1) * 64 and whose column index c has (c // 8) % (8) == j, that is the column's block of 8 tile rows, numbered c // 8, is held by column group j; live slots name distinct tiles with r >= c; slots at or beyond the count hold in-range indices that must be ignored. `tile_cols`: see tile_rows; the same slots. `tile_counts`: some lists are full in every draw; lists near the top of the triangle hold few tiles.
All inputs are finite; a program needn't handle non-finite values.
Results may differ from a plain program's by a relative error of at most 0.001.
Values may be sent and summed in bfloat16 or wider, within the bound.
A program may use at most 64 MiB of HBM per device.

v0:
```python
import math
import jax
import jax.numpy as jnp
from jax import lax
from jax.sharding import PartitionSpec as P


def shards(vectors, tile_vals, tile_rows, tile_cols, tile_counts):
    nrow = lax.axis_size("row")
    ncol = lax.axis_size("col")
    vlocal, width = vectors.shape
    tile = tile_vals.shape[-1]
    stretch = width // tile
    span = ncol * stretch
    colspan = nrow * stretch
    row_x = lax.all_gather(vectors, "col", axis=1, tiled=True)
    col_x = lax.all_gather(vectors, "row", axis=1, tiled=True)
    tiles = tile_vals[0, 0]
    rows = tile_rows[0, 0]
    cols = tile_cols[0, 0]
    count = tile_counts[0, 0]
    slots = jnp.arange(rows.shape[0], dtype=jnp.int32)
    live = slots < count
    mirror = live & (rows != cols)
    row_place = rows % span
    col_place = cols // span * stretch + cols % stretch
    row_blocks = row_x.reshape(vlocal, span, tile)
    col_blocks = col_x.reshape(vlocal, colspan, tile)
    picked_cols = jnp.take(col_blocks, col_place, axis=1)
    picked_rows = jnp.take(row_blocks, row_place, axis=1)
    down = jnp.einsum("tij,vtj->vti", tiles, picked_cols, preferred_element_type=jnp.float32)
    upper = jnp.einsum("tij,vti->vtj", tiles, picked_rows, preferred_element_type=jnp.float32)
    row_hit = (
        (row_place[None, :] == jnp.arange(span, dtype=jnp.int32)[:, None]) & live[None, :]
    ).astype(jnp.float32)
    col_hit = (
        (col_place[None, :] == jnp.arange(colspan, dtype=jnp.int32)[:, None]) & mirror[None, :]
    ).astype(jnp.float32)
    row_part = jnp.einsum("at,vti->vai", row_hit, down, precision=lax.Precision.HIGHEST).reshape(
        vlocal, span * tile
    )
    col_part = jnp.einsum("at,vti->vai", col_hit, upper, precision=lax.Precision.HIGHEST).reshape(
        vlocal, colspan * tile
    )
    row_whole = lax.psum(row_part, "col")
    col_whole = lax.psum(col_part, "row")
    row_share = lax.dynamic_slice_in_dim(row_whole, lax.axis_index("col") * width, width, 1)
    col_share = lax.dynamic_slice_in_dim(col_whole, lax.axis_index("row") * width, width, 1)
    image = row_share + col_share
    every_vector = lax.all_gather(vectors, "vec", axis=0, tiled=True)
    partial_gram = jnp.dot(
        every_vector.astype(jnp.float32), image.T, precision=lax.Precision.HIGHEST
    )
    gram = lax.psum(partial_gram, ("row", "col")) / math.sqrt(width * nrow * ncol)
    return (image.astype(jnp.bfloat16), gram)


def solution(mesh):
    return jax.shard_map(
        shards,
        mesh=mesh,
        in_specs=(
            P("vec", ("row", "col")),
            P("row", "col", None, None, None),
            P("row", "col", None),
            P("row", "col", None),
            P("row", "col"),
        ),
        out_specs=(P("vec", ("row", "col")), P(None, "vec")),
        check_vma=False,
    )
```

profile of v0, /device:TPU:8, one launch (start us, length us, event | category | flops | bytes accessed | tf_op | source)
XLA Modules:
  0.0 527.4 jit_solution(8425430569256399796)
XLA Ops:
  7.2 0.0 all-reduce.5.cloned.1.call-start
  7.2 28.5 %all_gather.10 = bf16[8,8192]{1,0:T(8,128)(2,1)S(1)} all-gather(bf16[8,1024]{1,0:T(8,128)(2,1)} %param.5), channel_id=1, replica_groups=mesh['row'=16,'col'=8,'vec'=2] {'col'}, dimensions={1}, use_global_device_ids=true | all-gather | bytes 147456 | tf_op jit(solution)/shard_map/all_gather | solution.py:16
  35.8 0.7 compare_select_fusion
  36.5 0.7 compare_and_fusion.1
  37.2 0.8 gather_fusion.1
  38.0 4.7 fusion
  42.7 0.4 copy.9
  43.8 0.6 convolution_bitcast_fusion
  44.5 0.2 copy.7
  44.7 1.1 copy.18
  45.8 0.0 all-reduce.5.cloned.1.call-update
  45.8 0.0 all-reduce.3.cloned.1.call-start
  45.9 20.7 %all_gather.9 = bf16[8,16384]{1,0:T(8,128)(2,1)S(1)} all-gather(bf16[8,1024]{1,0:T(8,128)(2,1)S(1)} %copy-done), channel_id=1, replica_groups=mesh['row'=16,'col'=8,'vec'=2] {'row'}, dimensions={1}, use_global_device_ids=true | all-gather | bytes 278528 | tf_op jit(solution)/shard_map/all_gather | solution.py:17
  66.6 0.8 gather_fusion
  67.4 6.8 %fusion.2 = f32[256,8,128]{2,1,0:T(8,128)S(1)} fusion(bf16[1,1,256,128,128]{4,3,2,1,0:T(8,128)(2,1)} %param.6, bf16[256,8,128]{2,1,0:T(8,128)(2,1)S(1)} %gather_fusion, pred[256]{0:T(512)(128)(4,1)S(1)} %get-tuple-element.2), kind=kOutput, calls=%fused_computation.4 | convolution fusion | flops 67371008 | bytes 9961728 | tf_op jit(solution)/shard_map/tij,vtj->vti/dot_general | solution.py:31
  74.2 0.6 convolution_bitcast_fusion.1
  74.8 0.9 copy.19
  75.7 5.9 %all_gather.11 = bf16[16,1024]{1,0:T(8,128)(2,1)S(1)} all-gather(bf16[8,1024]{1,0:T(8,128)(2,1)S(1)} %copy-done), channel_id=1, replica_groups=mesh['row'=16,'col'=8,'vec'=2] {'vec'}, dimensions={0}, use_global_device_ids=true | all-gather | bytes 49152 | tf_op jit(solution)/shard_map/all_gather | solution.py:50
  81.7 77.3 %all-reduce.5.cloned.1.call-done = f32[8,16384]{1,0:T(8,128)} async-done(((f32[8,16384]{1,0:T(8,128)}), f32[8,16384]{1,0:T(8,128)}) %all-reduce.5.cloned.1.call-update) | async-done | bytes 524304 | tf_op jit(solution)/shard_map/psum | solution.py:46
  159.0 79.9 %all-reduce.3.cloned.1.call-done = f32[8,8192]{1,0:T(8,128)} async-done(((f32[8,8192]{1,0:T(8,128)}), f32[8,8192]{1,0:T(8,128)}) %all-reduce.3.cloned.1.call-update) | async-done | bytes 262160 | tf_op jit(solution)/shard_map/psum | solution.py:45
  238.9 0.9 convolution_bitcast_fusion.2
  239.8 278.8 %psum.23 = f32[16,8]{0,1:T(8,128)S(1)} all-reduce(f32[16,8]{0,1:T(8,128)S(1)} %convolution_bitcast_fusion.2), channel_id=1, replica_groups=mesh['row'=16,'col'=8,'vec'=2] {'row','col'}, use_global_device_ids=true, to_apply=%region_2.3 | all-reduce | flops 128 | bytes 1024 | tf_op jit(solution)/shard_map/psum | solution.py:54
  518.6 0.6 broadcast_multiply_fusion
  519.2 1.4 fusion.25
  (12 shorter events, 0.1 us)
Async XLA Ops:
  7.2 36.6 %copy-start.1 = (s32[1,1,256]{2,1,0:T(1,128)S(1)}, s32[1,1,256]{2,1,0:T(1,128)}, u32[]{:S(2)}) copy-start(s32[1,1,256]{2,1,0:T(1,128)} %param.7) | copy-start | bytes 3076
  7.2 36.6 %copy-start.2 = (s32[1,1,256]{2,1,0:T(1,128)S(1)}, s32[1,1,256]{2,1,0:T(1,128)}, u32[]{:S(2)}) copy-start(s32[1,1,256]{2,1,0:T(1,128)} %param.8) | copy-start | bytes 3076
  7.2 151.8 %all-reduce.5.cloned.1.call-start = ((), (), s32[]{:S(2)}) async-start(), calls=%async_computation.1 | async-start | bytes 1048576 | tf_op jit(solution)/shard_map/psum | solution.py:46
  38.0 7.9 %copy-start = (bf16[8,1024]{1,0:T(8,128)(2,1)S(1)}, bf16[8,1024]{1,0:T(8,128)(2,1)}, u32[]{:S(2)}) copy-start(bf16[8,1024]{1,0:T(8,128)(2,1)} %param.5) | copy-start | bytes 49156
  45.8 193.1 %all-reduce.3.cloned.1.call-start = ((), (), s32[]{:S(2)}) async-start(), calls=%async_computation | async-start | bytes 524288 | tf_op jit(solution)/shard_map/psum | solution.py:45
Sparse Core Ops, SparseCore 0:
  45.9 113.0 all-reduce.4
  161.6 77.2 all-reduce.2
where the time goes:
time: 528 us; the launch traced here: 527 us
  blocking collectives  334 us (63%)
  waiting for transfers between devices  157 us (30%)
  between operations  14.8 us (3%)
  matrix products  13.7 us (3%)
    psum x1, blocking collectives, shards(): lax.psum(partial_gram, ('row', 'col')) / math.sqrt(width * nrow * ncol)  279 us
    psum x1, waiting for transfers between devices, shards(): row_whole = lax.psum(row_part, 'col')  79.9 us
    psum x1, waiting for transfers between devices, shards(): col_whole = lax.psum(col_part, 'row')  77.3 us
    all_gather x1, blocking collectives, shards(): row_x = lax.all_gather(vectors, 'col', axis=1, tiled=True)  28.5 us
    all_gather x1, blocking collectives, shards(): col_x = lax.all_gather(vectors, 'row', axis=1, tiled=True)  20.7 us
  transfers between devices with their start and end apart: 2, of which 2 were waited for; matrix products, arithmetic and copies ran while one was open for 2% of the time, Pallas kernels for 0%

commit v1 on v0

--- a/solution.py
+++ b/solution.py
@@ -51,7 +51,7 @@
     partial_gram = jnp.dot(
         every_vector.astype(jnp.float32), image.T, precision=lax.Precision.HIGHEST
     )
-    gram = lax.psum(partial_gram, ("row", "col")) / math.sqrt(width * nrow * ncol)
+    gram = lax.psum(lax.psum(partial_gram, "row"), "col") / math.sqrt(width * nrow * ncol)
     return (image.astype(jnp.bfloat16), gram)
 
 

time: 528 us -> 292 us (0.55)
  blocking collectives: 334 us -> 97.5 us
    psum x1 -> x2, blocking collectives: 279 us -> 42.4 us  [the longest x1 23.6 us: shards(): lax.psum(partial_gram, 'row')]
  transfers between devices with their start and end apart: 2 -> 2, of which waited for: 2 -> 2; matrix products, arithmetic and copies ran while one was open for 2% -> 3% of each run, Pallas kernels for 0% -> 0%
where the time goes in v1:
time: 292 us; the launch traced here: 291 us
  waiting for transfers between devices  157 us (54%)
  blocking collectives  97.5 us (33%)
  between operations  14.8 us (5%)
  matrix products  13.7 us (5%)
  local copies, waits for them, and re-layouts  4.24 us (1%)
  other arithmetic  3.42 us (1%)
    psum x1, waiting for transfers between devices, shards(): row_whole = lax.psum(row_part, 'col')  79.9 us
    psum x1, waiting for transfers between devices, shards(): col_whole = lax.psum(col_part, 'row')  77.3 us
    all_gather x1, blocking collectives, shards(): row_x = lax.all_gather(vectors, 'col', axis=1, tiled=True)  28.5 us
    psum x1, blocking collectives, shards(): lax.psum(partial_gram, 'row')  23.6 us
    all_gather x1, blocking collectives, shards(): col_x = lax.all_gather(vectors, 'row', axis=1, tiled=True)  20.7 us
    psum x1, blocking collectives, shards(): lax.psum(lax.psum(partial_gram, 'row'), 'col')  18.8 us
    dot_general x1, matrix products, shards(): jnp.einsum('tij,vtj->vti', tiles, picked_cols, preferred_element_type=jnp...  6.82 us
    all_gather x1, blocking collectives, shards(): every_vector = lax.all_gather(vectors, 'vec', axis=0, tiled=True)  5.91 us
  transfers between devices with their start and end apart: 2, of which 2 were waited for; matrix products, arithmetic and copies ran while one was open for 3% of the time, Pallas kernels for 0%

profile of v1, /device:TPU:8, one launch (start us, length us, event | category | flops | bytes accessed | tf_op | source)
XLA Modules:
  0.0 291.0 jit_solution(347598166588776884)
XLA Ops:
  7.2 0.0 all-reduce.5.cloned.1.call-start
  7.2 28.5 %all_gather.10 = bf16[8,8192]{1,0:T(8,128)(2,1)S(1)} all-gather(bf16[8,1024]{1,0:T(8,128)(2,1)} %param.5), channel_id=1, replica_groups=mesh['row'=16,'col'=8,'vec'=2] {'col'}, dimensions={1}, use_global_device_ids=true | all-gather | bytes 147456 | tf_op jit(solution)/shard_map/all_gather | solution.py:16
  35.8 0.7 compare_select_fusion
  36.5 0.7 compare_and_fusion.1
  37.2 0.8 gather_fusion.1
  38.0 4.7 %fusion = f32[256,8,128]{2,1,0:T(8,128)S(1)} fusion(bf16[1,1,256,128,128]{4,3,2,1,0:T(8,128)(2,1)} %param.6, bf16[256,8,128]{2,1,0:T(8,128)(2,1)S(1)} %gather_fusion.1, pred[256]{0:T(512)(128)(4,1)S(1)} %get-tuple-element.4), kind=kOutput, calls=%fused_computation.2 | convolution fusion | flops 67371008 | bytes 9961728 | tf_op jit(solution)/shard_map/tij,vti->vtj/dot_general | solution.py:32
  42.7 0.4 copy.9
  43.8 0.6 convolution_bitcast_fusion
  44.5 0.2 copy.7
  44.7 1.1 copy.18
  45.8 0.0 all-reduce.3.cloned.1.call-start
  45.9 20.7 %all_gather.9 = bf16[8,16384]{1,0:T(8,128)(2,1)S(1)} all-gather(bf16[8,1024]{1,0:T(8,128)(2,1)S(1)} %copy-done), channel_id=1, replica_groups=mesh['row'=16,'col'=8,'vec'=2] {'row'}, dimensions={1}, use_global_device_ids=true | all-gather | bytes 278528 | tf_op jit(solution)/shard_map/all_gather | solution.py:17
  66.6 0.8 gather_fusion
  67.4 6.8 %fusion.2 = f32[256,8,128]{2,1,0:T(8,128)S(1)} fusion(bf16[1,1,256,128,128]{4,3,2,1,0:T(8,128)(2,1)} %param.6, bf16[256,8,128]{2,1,0:T(8,128)(2,1)S(1)} %gather_fusion, pred[256]{0:T(512)(128)(4,1)S(1)} %get-tuple-element.2), kind=kOutput, calls=%fused_computation.4 | convolution fusion | flops 67371008 | bytes 9961728 | tf_op jit(solution)/shard_map/tij,vtj->vti/dot_general | solution.py:31
  74.2 0.6 convolution_bitcast_fusion.1
  74.9 0.9 copy.19
  75.8 5.9 %all_gather.11 = bf16[16,1024]{1,0:T(8,128)(2,1)S(1)} all-gather(bf16[8,1024]{1,0:T(8,128)(2,1)S(1)} %copy-done), channel_id=1, replica_groups=mesh['row'=16,'col'=8,'vec'=2] {'vec'}, dimensions={0}, use_global_device_ids=true | all-gather | bytes 49152 | tf_op jit(solution)/shard_map/all_gather | solution.py:50
  81.7 77.3 %all-reduce.5.cloned.1.call-done = f32[8,16384]{1,0:T(8,128)} async-done(((f32[8,16384]{1,0:T(8,128)}), f32[8,16384]{1,0:T(8,128)}) %all-reduce.5.cloned.1.call-update) | async-done | bytes 524304 | tf_op jit(solution)/shard_map/psum | solution.py:46
  159.0 79.9 %all-reduce.3.cloned.1.call-done = f32[8,8192]{1,0:T(8,128)} async-done(((f32[8,8192]{1,0:T(8,128)}), f32[8,8192]{1,0:T(8,128)}) %all-reduce.3.cloned.1.call-update) | async-done | bytes 262160 | tf_op jit(solution)/shard_map/psum | solution.py:45
  238.9 0.9 convolution_bitcast_fusion.2
  239.8 23.6 %psum.30 = f32[16,8]{0,1:T(8,128)S(1)} all-reduce(f32[16,8]{0,1:T(8,128)S(1)} %convolution_bitcast_fusion.2), channel_id=1, replica_groups=mesh['row'=16,'col'=8,'vec'=2] {'row'}, use_global_device_ids=true, to_apply=%region_2.3 | all-reduce | flops 128 | bytes 1024 | tf_op jit(solution)/shard_map/psum | solution.py:54
  263.4 18.8 %psum.31 = f32[16,8]{0,1:T(8,128)S(1)} all-reduce(f32[16,8]{0,1:T(8,128)S(1)} %psum.30), channel_id=1, replica_groups=mesh['row'=16,'col'=8,'vec'=2] {'col'}, use_global_device_ids=true, to_apply=%region_3.4 | all-reduce | flops 128 | bytes 1024 | tf_op jit(solution)/shard_map/psum | solution.py:54
  282.2 0.6 broadcast_multiply_fusion
  282.8 1.4 fusion.25
  (13 shorter events, 0.1 us)
Async XLA Ops:
  7.2 36.6 %copy-start.1 = (s32[1,1,256]{2,1,0:T(1,128)S(1)}, s32[1,1,256]{2,1,0:T(1,128)}, u32[]{:S(2)}) copy-start(s32[1,1,256]{2,1,0:T(1,128)} %param.7) | copy-start | bytes 3076
  7.2 36.6 %copy-start.2 = (s32[1,1,256]{2,1,0:T(1,128)S(1)}, s32[1,1,256]{2,1,0:T(1,128)}, u32[]{:S(2)}) copy-start(s32[1,1,256]{2,1,0:T(1,128)} %param.8) | copy-start | bytes 3076
  7.2 151.8 %all-reduce.5.cloned.1.call-start = ((), (), s32[]{:S(2)}) async-start(), calls=%async_computation.1 | async-start | bytes 1048576 | tf_op jit(solution)/shard_map/psum | solution.py:46
  38.0 7.9 %copy-start = (bf16[8,1024]{1,0:T(8,128)(2,1)S(1)}, bf16[8,1024]{1,0:T(8,128)(2,1)}, u32[]{:S(2)}) copy-start(bf16[8,1024]{1,0:T(8,128)(2,1)} %param.5) | copy-start | bytes 49156
  45.8 193.1 %all-reduce.3.cloned.1.call-start = ((), (), s32[]{:S(2)}) async-start(), calls=%async_computation | async-start | bytes 524288 | tf_op jit(solution)/shard_map/psum | solution.py:45
Sparse Core Ops, SparseCore 0:
  45.9 113.0 all-reduce.4
  161.6 77.2 all-reduce.2
